TPU v7x, 512 devices: a whole 4x4x16 slice. The times are simulated.
512 devices in a mesh: lon: 32 (over z_lo, x), ch: 16 (over z_hi, y, core).
Axes of the slice: x: 4, y: 4, z: 16 (z_hi: 2, z_lo: 8; z = z_hi * 8 + z_lo), core: 2. Of those that a mesh axis runs over, the one named last changes fastest.
Arguments:
- inputs: bfloat16 [1, 4, 48, 64, 512], P(None, None, None, 'lon', 'ch'), may hold values from -6 to 6
- grad_out: bfloat16 [1, 4, 48, 64, 512], P(None, None, None, 'lon', 'ch'), may hold values from -6 to 6
- kernel: bfloat16 [3, 3, 3, 512, 512], P(None, None, None, 'ch'), may hold values from -0.0546875 to 0.0546875
Outputs:
- grad_in: bfloat16 [1, 4, 48, 64, 512], P(None, None, None, 'lon', 'ch')
- grad_kernel: float32 [3, 3, 3, 512, 512], P(None, None, None, 'ch', 'lon')
All inputs are finite; a program needn't handle non-finite values.
Results may differ from a plain program's by a relative error of at most 0.0012.
Values may be sent and summed in bfloat16 or wider, within the bound.
A program may use at most 64 MiB of HBM per device.

v0:
```python
import math
import jax
import jax.numpy as jnp
from jax import lax
from jax.sharding import PartitionSpec as P


def with_halo(cells, sides, width):
    for axis, dim in sides:
        count = lax.axis_size(axis)
        head = lax.slice_in_dim(cells, 0, width, axis=dim)
        tail = lax.slice_in_dim(cells, cells.shape[dim] - width, cells.shape[dim], axis=dim)
        cells = jnp.concatenate(
            [
                lax.ppermute(tail, axis, [(i, (i + 1) % count) for i in range(count)]),
                cells,
                lax.ppermute(head, axis, [((i + 1) % count, i) for i in range(count)]),
            ],
            axis=dim,
        )
    return cells


def contract_rows(left, right):
    return lax.dot_general(
        left, right, (((0,), (0,)), ((), ())), preferred_element_type=jnp.float32
    )


def tap_product(grad_all, kernel, step_t):
    out_width = grad_all.shape[4]
    cin_loc = kernel.shape[3]
    stacked = kernel[step_t].transpose(3, 0, 1, 2).reshape(out_width, 9 * cin_loc)
    product = jnp.dot(grad_all.reshape(-1, out_width), stacked, preferred_element_type=jnp.float32)
    return product.reshape(grad_all.shape[:4] + (3, 3, cin_loc))


def body(inputs, grad_out, kernel):
    batches, frames, lat_cells, lon_cols, cin_loc = inputs.shape
    lon_cells = lon_cols * lax.axis_size("lon")
    rscale = 1.0 / math.sqrt(batches * frames * lat_cells * lon_cells)
    grad_ext = with_halo(grad_out, (("lon", 3),), 1)
    grad_all = lax.all_gather(grad_ext, "ch", axis=4, tiled=True)
    out_width = grad_all.shape[4]
    accum_dx = jnp.zeros((batches, frames, lat_cells, lon_cols, cin_loc), jnp.float32)
    for step_t in range(3):
        product = tap_product(grad_all, kernel, step_t)
        padded = jnp.pad(product, ((0, 0), (1, 1), (1, 1), (0, 0), (0, 0), (0, 0), (0, 0)))
        for step_h in range(3):
            for step_w in range(3):
                accum_dx = (
                    accum_dx
                    + padded[
                        :,
                        2 - step_t : 2 - step_t + frames,
                        2 - step_h : 2 - step_h + lat_cells,
                        2 - step_w : 2 - step_w + lon_cols,
                        step_h,
                        step_w,
                        :,
                    ]
                )
    grad_in = accum_dx.astype(jnp.bfloat16)
    tap_terms = []
    shifted = jnp.stack(
        [
            jnp.pad(inputs, ((0, 0), (0, 0), (0, 0), (2 - step_w, step_w), (0, 0)))
            for step_w in range(3)
        ],
        axis=4,
    )
    x_pad = jnp.pad(shifted, ((0, 0), (1, 1), (1, 1), (0, 0), (0, 0), (0, 0)))
    flat_grad = grad_all.reshape(-1, out_width)
    for step_t in range(3):
        x_block = jnp.stack(
            [
                x_pad[:, step_t : step_t + frames, step_h : step_h + lat_cells]
                for step_h in range(3)
            ],
            axis=4,
        )
        tap_terms.append(
            contract_rows(x_block.reshape(-1, 9 * cin_loc), flat_grad).reshape(
                3, 3, cin_loc, out_width
            )
        )
    weight_terms = jnp.stack(tap_terms) * rscale
    grad_kernel = lax.psum_scatter(weight_terms, "lon", scatter_dimension=4, tiled=True)
    return (grad_in, grad_kernel)


def solution(mesh):
    return jax.shard_map(
        body,
        mesh=mesh,
        in_specs=(
            P(None, None, None, "lon", "ch"),
            P(None, None, None, "lon", "ch"),
            P(None, None, None, "ch", None),
        ),
        out_specs=(P(None, None, None, "lon", "ch"), P(None, None, None, "ch", "lon")),
        check_vma=False,
    )
```

profile of v0, /device:TPU:8, one launch (start us, length us, event | category | flops | bytes accessed | tf_op | source)
XLA Modules:
  0.0 632.7 jit_solution(9007344255820453416)
XLA Ops:
  9.5 15.3 %collective-permute-start.1 = (bf16[1,4,48,1,32]{2,3,1,0,4:T(2,128)(2,1)}, bf16[1,4,48,1,32]{2,3,1,0,4:T(2,128)(2,1)}, u32[]{:S(2)}, u32[]{:S(2)}) collective-permute-start(bf16[1,4,48,1,32]{2,3,1,0,4:T(2,128)(2,1)} %get-tuple-element.22), channel_id=1, source_target_pairs={{16,0},{32,16},{48,32},{64,48},{80,64},{96,80},{112,96},{128,112},... | collective-permute-start | bytes 36872 | tf_op jit(solution)/shard_map/ppermute | solution.py:17
  24.8 1.9 collective-permute-start
  26.7 1.0 pad_bitcast_fusion.2
  28.7 2.0 pad_maximum_fusion
  31.0 2.1 copy.59
  33.1 2.3 reshape.403
  35.4 2.0 copy.60
  37.4 2.1 copy.57
  39.5 2.3 reshape.401
  41.8 2.1 copy.58
  43.8 2.1 copy.54
  45.9 1.3 reshape.398
  47.2 1.0 copy.55
  48.2 1.1 pad_maximum_fusion.4
  49.4 49.3 %all_gather.3 = bf16[1,4,48,4,512]{2,3,1,0,4:T(4,128)(2,1)S(1)} all-gather(bf16[1,4,48,4,32]{2,3,1,0,4:T(4,128)(2,1)S(1)} %pad_maximum_fusion.4), channel_id=1, replica_groups=mesh['lon'=32,'ch'=16] {'ch'}, dimensions={4}, use_global_device_ids=true | all-gather | bytes 835584 | tf_op jit(solution)/shard_map/all_gather | solution.py:43
  98.7 2.9 copy.56
  101.5 1.6 reshape.421
  104.9 1.4 maximum_multiply_fusion
  106.3 8.7 %copy.61 = f32[3,3,3,32,512]{3,2,1,0,4:T(4,128)} copy(f32[3,3,3,32,512]{4,3,2,1,0:T(8,128)} %maximum_multiply_fusion) | data formatting | bytes 3538944 | tf_op jit(solution)/shard_map/mul | solution.py:87
  115.0 1.3 dynamic-slice
  116.9 1.8 copy.43
  118.8 1.8 convolution_bitcast_fusion
  122.2 1.2 fusion.61
  123.4 500.7 %all-reduce.10.cloned.1.call-done = f32[3,3,3,32,512]{3,2,1,0,4:T(4,128)} async-done(((f32[3,3,3,32,512]{3,2,1,0,4:T(4,128)}), f32[3,3,3,32,512]{3,2,1,0,4:T(4,128)}) %all-reduce.10.cloned.1.call-update) | async-done | bytes 1769488
  (32 shorter events, 8.5 us)
Async XLA Ops:
  7.2 617.0 %all-reduce.10.cloned.1.call-start = ((), (), s32[]{:S(2)}) async-start(), calls=%async_computation | async-start | bytes 18874368
  8.1 0.6 copy-start.5
  9.5 38.8 %collective-permute-start.1 = (bf16[1,4,48,1,32]{2,3,1,0,4:T(2,128)(2,1)}, bf16[1,4,48,1,32]{2,3,1,0,4:T(2,128)(2,1)}, u32[]{:S(2)}, u32[]{:S(2)}) collective-permute-start(bf16[1,4,48,1,32]{2,3,1,0,4:T(2,128)(2,1)} %get-tuple-element.22), channel_id=1, source_target_pairs={{16,0},{32,16},{48,32},{64,48},{80,64},{96,80},{112,96},{128,112},... | collective-permute-start | bytes 36872 | tf_op jit(solution)/shard_map/ppermute | solution.py:17
  24.8 23.4 %collective-permute-start = (bf16[1,4,48,1,32]{2,3,1,0,4:T(2,128)(2,1)}, bf16[1,4,48,1,32]{2,3,1,0,4:T(2,128)(2,1)}, u32[]{:S(2)}, u32[]{:S(2)}) collective-permute-start(bf16[1,4,48,1,32]{2,3,1,0,4:T(2,128)(2,1)} %get-tuple-element.21), channel_id=1, source_target_pairs={{0,16},{16,32},{32,48},{48,64},{64,80},{80,96},{96,112},{112,128},... | collective-permute-start | bytes 36872 | tf_op jit(solution)/shard_map/ppermute | solution.py:15
  33.1 4.3 copy-start.1
  39.5 4.4 copy-start
  45.9 2.3 copy-start.6
  98.7 4.4 copy-start.2
  103.1 1.0 copy-start.3
  103.1 1.4 copy-start.4
  118.8 1.8 copy-start.7
Sparse Core Ops, SparseCore 0:
  115.1 508.9 all-reduce.9
where the time goes:
time: 633 us
  waiting for transfers between devices  501 us (79%)
  blocking collectives  49.3 us (8%)
  local copies, waits for them, and re-layouts  39.7 us (6%)
  starting transfers between devices  17.3 us (3%)
  between operations  14.9 us (2%)
    unnamed x2, waiting for transfers between devices  501 us
    all_gather x1, blocking collectives, body(): grad_all = lax.all_gather(grad_ext, 'ch', axis=4, tiled=True)  49.3 us
    ppermute x1, starting transfers between devices, with_halo(): lax.ppermute(head, axis, [((i + 1) % count, i) for i in range(count)])  15.3 us
  transfers between devices with their start and end apart: 3, of which 1 were waited for; matrix products, arithmetic and copies ran while one was open for 5% of the time, Pallas kernels for 0%

commit v1 on v0

--- a/solution.py
+++ b/solution.py
@@ -40,7 +40,9 @@
     lon_cells = lon_cols * lax.axis_size("lon")
     rscale = 1.0 / math.sqrt(batches * frames * lat_cells * lon_cells)
     grad_ext = with_halo(grad_out, (("lon", 3),), 1)
-    grad_all = lax.all_gather(grad_ext, "ch", axis=4, tiled=True)
+    grad_all = jnp.concatenate(
+        lax.all_to_all(jnp.stack([grad_ext] * lax.axis_size("ch")), "ch", 0, 0), axis=4
+    )
     out_width = grad_all.shape[4]
     accum_dx = jnp.zeros((batches, frames, lat_cells, lon_cols, cin_loc), jnp.float32)
     for step_t in range(3):

time: 633 us -> 613 us (0.968)
  blocking collectives: 49.3 us -> 0 us
  local copies, waits for them, and re-layouts: 39.7 us -> 67.7 us
  starting transfers between devices: 17.3 us -> 28.2 us
  waiting for transfers between devices: 501 us -> 491 us
    all_gather x1 -> x0, blocking collectives: 49.3 us -> none  [body(): grad_all = lax.all_gather(grad_ext, 'ch', axis=4, tiled=True)]
    unnamed x2, waiting for transfers between devices: 501 us -> 477 us
    ppermute x1, waiting for transfers between devices: 0.01 us -> 12.6 us  [with_halo(): lax.ppermute(tail, axis, [(i, (i + 1) % count) for i in range(count)])]
    all_to_all x0 -> x1, starting transfers between devices: none -> 10.7 us  [body(): lax.all_to_all(jnp.stack([grad_ext] * lax.axis_size('ch')), 'ch', 0, 0)]
    reshape x1 -> x3, local copies, waits for them, and re-layouts: 1.56 us -> 11.4 us  [body(): jnp.concatenate(lax.all_to_all(jnp.stack([grad_ext] * lax.axis_size('ch')...]
    another operation x0 -> x2, local copies, waits for them, and re-layouts: none -> 9.3 us
    reshape x3, local copies, waits for them, and re-layouts: 5.82 us -> 12.4 us  [body(): x_block.reshape(-1, 9 * cin_loc)]
  transfers between devices with their start and end apart: 3 -> 4, of which waited for: 1 -> 3; matrix products, arithmetic and copies ran while one was open for 5% -> 7% of each run, Pallas kernels for 0% -> 0%
where the time goes in v1:
time: 613 us; the launch traced here: 612 us
  waiting for transfers between devices  491 us (80%)
  local copies, waits for them, and re-layouts  67.7 us (11%)
  starting transfers between devices  28.2 us (5%)
  between operations  14.9 us (2%)
  other arithmetic  6.84 us (1%)
    unnamed x2, waiting for transfers between devices  477 us
    ppermute x1, starting transfers between devices, with_halo(): lax.ppermute(head, axis, [((i + 1) % count, i) for i in range(count)])  15.3 us
    ppermute x1, waiting for transfers between devices, with_halo(): lax.ppermute(tail, axis, [(i, (i + 1) % count) for i in range(count)])  12.6 us
    reshape x3, local copies, waits for them, and re-layouts, body(): x_block.reshape(-1, 9 * cin_loc)  12.4 us
  transfers between devices with their start and end apart: 4, of which 3 were waited for; matrix products, arithmetic and copies ran while one was open for 7% of the time, Pallas kernels for 0%

profile of v1, /device:TPU:8, one launch (start us, length us, event | category | flops | bytes accessed | tf_op | source)
XLA Modules:
  0.0 612.4 jit_solution(14923154501753116178)
XLA Ops:
  8.0 15.3 %collective-permute-start.1 = (bf16[1,4,48,1,32]{2,4,3,1,0:T(8,128)(2,1)S(1)}, bf16[1,4,48,1,32]{2,4,3,1,0:T(8,128)(2,1)S(1)}, u32[]{:S(2)}, u32[]{:S(2)}) collective-permute-start(bf16[1,4,48,1,32]{2,4,3,1,0:T(8,128)(2,1)S(1)} %get-tuple-element.22), channel_id=1, source_target_pairs={{16,0},{32,16},{48,32},{64,48},{80,64},{96,80},{112,96},{128,112},... | collective-permute-start | bytes 36872 | tf_op jit(solution)/shard_map/ppermute | solution.py:17
  23.3 1.9 collective-permute-start
  25.2 12.6 %collective-permute-done = bf16[1,4,48,1,32]{2,4,3,1,0:T(8,128)(2,1)S(1)} collective-permute-done((bf16[1,4,48,1,32]{2,4,3,1,0:T(8,128)(2,1)S(1)}, bf16[1,4,48,1,32]{2,4,3,1,0:T(8,128)(2,1)S(1)}, u32[]{:S(2)}, u32[]{:S(2)}) %collective-permute-start) | collective-permute-done | bytes 12320 | tf_op jit(solution)/shard_map/ppermute | solution.py:15
  39.2 3.9 reshape.428
  43.1 10.7 %all-to-all-start = ((bf16[16,2,12288]{2,1,0:T(2,128)(2,1)}), bf16[16,2,12288]{2,1,0:T(2,128)(2,1)S(1)}, u32[]{:S(2)}, u32[]{:S(2)}) async-start(bf16[16,2,12288]{2,1,0:T(2,128)(2,1)} %reshape.428), calls=%async_computation | async-start | bytes 1572864 | tf_op jit(solution)/shard_map/all_to_all | solution.py:44
  54.9 1.9 fusion.6
  57.1 3.1 copy.53
  60.2 4.1 reshape.406
  65.3 2.2 pad_maximum_fusion
  67.5 3.1 copy.51
  70.6 4.1 reshape.404
  75.7 3.1 copy.48
  78.8 4.1 reshape.402
  85.1 3.1 reshape.429
  88.1 2.2 bitcast_bitcast_fusion
  90.4 5.5 copy.50
  95.9 4.6 reshape.424
  102.3 1.4 maximum_multiply_fusion
  103.8 8.7 %copy.55 = f32[3,3,3,32,512]{3,2,1,0,4:T(4,128)} copy(f32[3,3,3,32,512]{4,3,2,1,0:T(8,128)} %maximum_multiply_fusion) | data formatting | bytes 3538944 | tf_op jit(solution)/shard_map/mul | solution.py:89
  112.5 1.3 dynamic-slice
  114.4 3.7 copy.37
  118.1 4.7 reshape.420
  125.1 1.2 fusion.61
  126.3 477.5 %all-reduce.10.cloned.1.call-done = f32[3,3,3,32,512]{3,2,1,0,4:T(4,128)} async-done(((f32[3,3,3,32,512]{3,2,1,0,4:T(4,128)}), f32[3,3,3,32,512]{3,2,1,0,4:T(4,128)}) %all-reduce.10.cloned.1.call-update) | async-done | bytes 1769488
  (31 shorter events, 13.6 us)
Async XLA Ops:
  8.0 17.3 %collective-permute-start.1 = (bf16[1,4,48,1,32]{2,4,3,1,0:T(8,128)(2,1)S(1)}, bf16[1,4,48,1,32]{2,4,3,1,0:T(8,128)(2,1)S(1)}, u32[]{:S(2)}, u32[]{:S(2)}) collective-permute-start(bf16[1,4,48,1,32]{2,4,3,1,0:T(8,128)(2,1)S(1)} %get-tuple-element.22), channel_id=1, source_target_pairs={{16,0},{32,16},{48,32},{64,48},{80,64},{96,80},{112,96},{128,112},... | collective-permute-start | bytes 36872 | tf_op jit(solution)/shard_map/ppermute | solution.py:17
  23.3 14.5 %collective-permute-start = (bf16[1,4,48,1,32]{2,4,3,1,0:T(8,128)(2,1)S(1)}, bf16[1,4,48,1,32]{2,4,3,1,0:T(8,128)(2,1)S(1)}, u32[]{:S(2)}, u32[]{:S(2)}) collective-permute-start(bf16[1,4,48,1,32]{2,4,3,1,0:T(8,128)(2,1)S(1)} %get-tuple-element.21), channel_id=1, source_target_pairs={{0,16},{16,32},{32,48},{48,64},{64,80},{80,96},{96,112},{112,128},... | collective-permute-start | bytes 36872 | tf_op jit(solution)/shard_map/ppermute | solution.py:15
  39.2 14.8 %copy-start.4 = (bf16[1,4,48,2,32]{2,4,3,1,0:T(8,128)(2,1)S(1)}, bf16[1,4,48,2,32]{2,4,3,1,0:T(8,128)(2,1)}, u32[]{:S(2)}) copy-start(bf16[1,4,48,2,32]{2,4,3,1,0:T(8,128)(2,1)} %param.3) | copy-start | bytes 73732
  43.1 42.0 %all-to-all-start = ((bf16[16,2,12288]{2,1,0:T(2,128)(2,1)}), bf16[16,2,12288]{2,1,0:T(2,128)(2,1)S(1)}, u32[]{:S(2)}, u32[]{:S(2)}) async-start(bf16[16,2,12288]{2,1,0:T(2,128)(2,1)} %reshape.428), calls=%async_computation | async-start | bytes 1572864 | tf_op jit(solution)/shard_map/all_to_all | solution.py:44
  53.7 550.0 %all-reduce.10.cloned.1.call-start = ((), (), s32[]{:S(2)}) async-start(), calls=%async_computation.1 | async-start | bytes 18874368
  95.9 4.7 copy-start
  100.5 1.0 copy-start.1
  100.5 1.4 copy-start.2
  118.1 4.7 copy-start.3
Sparse Core Ops, SparseCore 0:
  112.6 491.1 all-reduce.9
